TPU v7x, 256 devices: a whole 4x4x8 slice. The times are simulated.
256 devices in a mesh: ep: 2 (over x_hi), row: 16 (over y, x_lo, core), col: 8 (over z).
Axes of the slice: x: 4 (x_hi: 2, x_lo: 2; x = x_hi * 2 + x_lo), y: 4, z: 8, core: 2. Of those that a mesh axis runs over, the one named last changes fastest.
Arguments:
- design: bfloat16 [1024, 16384], P(('ep', 'col'), 'row'), may hold values from -0.09375 to 0.09375
- taps: float32 [64], replicated, may hold values from -1 to 1
- tap_count: int32 [1024], P(('ep', 'col')), may hold values from 32 to 64
- order: int32 [16384], P('row'), may hold values from 0 to 16383, as said below
- regular: float32 [16384], replicated, may hold values from 0.5 to 2
Outputs:
- factored: float32 [16384, 16384], P('row', ('ep', 'col'))
Inputs may be any that keep to these rules, and one draw needn't show every extreme that they name: `order`: a permutation of 0 to 16383 that maps every index into its own aligned group of 128.
All inputs are finite; a program needn't handle non-finite values.
Results may differ from a plain program's by a relative error of at most 0.0037.
Values may be sent and summed in bfloat16 or wider, within the bound.
A program may use at most 64 MiB of HBM per device.

v0:
```python
import functools

import jax
import jax.numpy as jnp
from jax import lax
from jax.experimental import pallas as pl
from jax.experimental.pallas import tpu as pltpu
from jax.sharding import PartitionSpec as P

MESH = pl.DeviceIdType.MESH
F32 = jnp.float32
BF16 = jnp.bfloat16
HIGHEST = lax.Precision.HIGHEST
PB = 128
PAN = 512
EB = 64
NE = 16
HALF = 256


def dot_nn(a, b, precision=None):
    return lax.dot_general(
        a, b, (((1,), (0,)), ((), ())), precision=precision, preferred_element_type=F32
    )


def dot_nt(a, b, precision=None):
    return lax.dot_general(
        a, b, (((1,), (1,)), ((), ())), precision=precision, preferred_element_type=F32
    )


def split2(x):
    high = x.astype(BF16)
    return high, (x - high.astype(F32)).astype(BF16)


def lane_bcast(v, j):
    return jnp.broadcast_to(v[:, j : j + 1], (8, 128))


def row_bcast(v, k):
    return jnp.broadcast_to(v[k : k + 1, :], (8, 128))


def invert_factor(groups):
    sub = lax.broadcasted_iota(jnp.int32, (8, 128), 0)
    lane = lax.broadcasted_iota(jnp.int32, (8, 128), 1)
    a = list(groups)
    g = [jnp.where(lane == sub + 8 * q, 1.0, 0.0).astype(F32) for q in range(16)]
    for p in range(16):
        v = a[p]
        c = [lane_bcast(v, 8 * p + k) for k in range(8)]
        s = [[None] * 8 for _ in range(8)]
        for k in range(8):
            for i in range(k, 8):
                s[i][k] = row_bcast(c[k], i)
        rinv = [None] * 8
        lcol = [None] * 8
        dvec = None
        gp = g[p]
        for k in range(8):
            r = 1.0 / s[k][k]
            rinv[k] = r
            for i in range(k + 1, 8):
                m = s[i][k] * r
                for j in range(k + 1, i + 1):
                    s[i][j] = s[i][j] - m * s[j][k]
            if k < 7:
                lcol[k] = jnp.where(sub > k, c[k] * r, 0.0)
                for m in range(k + 1, 8):
                    c[m] = c[m] - lcol[k] * s[m][k]
            dvec = s[k][k] if dvec is None else jnp.where(sub == k, s[k][k], dvec)
        vrow = [None] * 8
        grow = [None] * 8
        for k in range(8):
            vrow[k] = row_bcast(v, k)
            grow[k] = row_bcast(gp, k)
            if k < 7:
                v = v - lcol[k] * vrow[k]
                gp = gp - lcol[k] * grow[k]
        for q in range(p + 1, 16):
            d = [lane_bcast(a[q], 8 * p + k) for k in range(8)]
            for k in range(8):
                d[k] = d[k] * rinv[k]
                for m in range(k + 1, 8):
                    d[m] = d[m] - d[k] * s[m][k]
            aq, gq = a[q], g[q]
            for k in range(8):
                aq = aq - d[k] * vrow[k]
                gq = gq - d[k] * grow[k]
            a[q], g[q] = aq, gq
        g[p] = gp * lax.rsqrt(dvec)
    return g


def factor_step(s, w, b):
    n = s.shape[0]
    lo, hi = 128 * b, 128 * b + 128
    g = invert_factor([s[lo + 8 * q : lo + 8 * q + 8, lo:hi] for q in range(16)])
    for q in range(16):
        w[lo + 8 * q : lo + 8 * q + 8, lo:hi] = g[q]
    inv = w[lo:hi, lo:hi]
    if b > 0:
        w[lo:hi, :lo] = dot_nn(inv, w[lo:hi, :lo], HIGHEST)
    if hi < n:
        below = dot_nt(s[hi:, lo:hi], inv, HIGHEST)
        s[hi:, hi:] = s[hi:, hi:] - dot_nt(below, below, HIGHEST)
        w[hi:, :hi] = w[hi:, :hi] - dot_nn(below, w[lo:hi, :hi], HIGHEST)


def gather_kernel(
    design_ref, taps_ref, count_ref, order_ref, reg_ref,
    frt_ref, fc_ref, rr_ref, rct_ref,
    xr, xc, rp, po, pf, pft, smat, wmat,
    bx_s, bx_r, br_s, br_r, p1_s, p1_r, c1_s, c1_r, xs, xq, rs, rq, c2_s, c2_r, cc_s, cc_r, cp_s, cp_r,
):
    ep = lax.axis_index("ep")
    row = lax.axis_index("row")
    col = lax.axis_index("col")
    core = row % 2
    e_own = ep * 8 + col
    group = e_own
    up, down = (col + 1) % 8, (col + 7) % 8
    to_up = {"ep": ep, "row": row, "col": up}
    to_down = {"ep": ep, "row": row, "col": down}
    to_ep = {"ep": 1 - ep, "row": row, "col": col}
    core_row = row - core + (1 - core)
    xlo = (row // 2) % 2
    x_row = row + 2 - 4 * xlo
    yup_row, ydown_row = (row + 4) % 16, (row + 12) % 16
    plane = lambda r: {"ep": ep, "row": r, "col": col}
    is_self = jnp.logical_and(row == group, core == ep)

    barrier = pltpu.get_barrier_semaphore()
    for dev in (to_up, to_down, to_ep, plane(core_row), plane(x_row), plane(yup_row), plane(ydown_row)):
        pl.semaphore_signal(barrier, inc=1, device_id=dev, device_id_type=MESH)

    @pl.when(row != 0)
    def _():
        pl.semaphore_signal(barrier, inc=1, device_id=plane(0), device_id_type=MESH)

    for z in range(8):
        mine = jnp.logical_and(is_self, col == z)

        @pl.when(jnp.logical_not(mine))
        def _():
            pl.semaphore_signal(
                barrier, inc=1, device_id={"ep": core, "row": group, "col": z}, device_id_type=MESH
            )

    local = order_ref[...] % PB
    kk = lax.broadcasted_iota(jnp.int32, (PB, 1024), 0)
    one_hot = jnp.where(kk == local, 1.0, 0.0).astype(BF16)
    own = e_own + 1
    for g in range(8):
        part = dot_nn(design_ref[:, g * PB : (g + 1) * PB], one_hot[:, g * PB : (g + 1) * PB])
        xr[own, :, g * PB : (g + 1) * PB] = part.astype(BF16)
    ii = lax.broadcasted_iota(jnp.int32, (EB, 128), 0)
    jj = lax.broadcasted_iota(jnp.int32, (EB, 128), 1)
    lag = ii + EB - jj
    ti = lax.broadcasted_iota(jnp.int32, (EB, EB), 0)
    tj = lax.broadcasted_iota(jnp.int32, (EB, EB), 1)
    counts = jnp.sum(jnp.where(ti == tj, count_ref[...].astype(F32), 0.0), axis=1, keepdims=True)
    band = jnp.zeros((EB, 128), F32)
    for t in range(taps_ref.shape[0]):
        band = jnp.where(lag == t, taps_ref[t], band)
    band = jnp.where(lag.astype(F32) < counts, band, 0.0)
    rp[own, :, HALF:] = band.astype(BF16)
    xr[0] = jnp.zeros(xr.shape[1:], BF16)
    rp[0] = jnp.zeros(rp.shape[1:], BF16)
    po[0] = jnp.zeros(po.shape[1:], BF16)
    for q in range(8):
        xc[q, 0] = jnp.zeros((EB, PB), BF16)

    @pl.when(row == 0)
    def _():
        rp[own, :, :HALF] = xr[own, :, :HALF]

    pl.semaphore_wait(
        barrier, 7 + 8 + jnp.where(row == 0, 15, 0) - jnp.where(is_self, 1, 0)
    )

    sends = []

    def remote(src, dst, s_sem, r_sem, dev):
        return pltpu.make_async_remote_copy(
            src_ref=src, dst_ref=dst, send_sem=s_sem, recv_sem=r_sem, device_id=dev, device_id_type=MESH
        )

    def send(src, dst, s_sem, r_sem, dev):
        copy = remote(src, dst, s_sem, r_sem, dev)
        copy.start()
        sends.append(copy)

    @pl.when(row == 0)
    def _():
        for t in range(1, 16):
            half = t % 2
            remote(
                xr.at[own, :, half * HALF : (half + 1) * HALF], rp.at[own, :, 0:HALF],
                p1_s.at[t - 1], p1_r, plane(t),
            ).start()

    eps = (ep, 1 - ep)

    def ring_origin(direction, s):
        return (col + 8 - s) % 8 if direction == 0 else (col + s) % 8

    def ring_piece(buf, k, z, direction, s):
        slot = eps[k] * 8 + z + 1
        if s < 3:
            return buf.at[slot]
        return buf.at[slot, pl.ds(32 * direction, 32)]

    def ring_send(buf, ssem, rsem, direction, s, k):
        piece = ring_piece(buf, k, ring_origin(direction, s), direction, s)
        send(piece, piece, ssem.at[direction, s, k], rsem.at[direction, s, k], (to_up, to_down)[direction])

    def ring_wait(buf, ssem, rsem, direction, s, k):
        piece = ring_piece(buf, k, ring_origin(direction, s + 1), direction, s)
        remote(piece, piece, ssem.at[direction, s, k], rsem.at[direction, s, k], to_up).wait_recv()

    for direction in range(2):
        ring_send(xr, xs, xq, direction, 0, 0)
    for q in range(8):
        src = xr.at[own, :, q * PB : (q + 1) * PB]
        dst = xc.at[q, own]
        mine = jnp.logical_and(is_self, row // 2 == q)

        @pl.when(jnp.logical_not(mine))
        def _():
            remote(
                src, dst, c1_s.at[q], c1_r.at[col],
                {"ep": row // 8, "row": 2 * q + ep, "col": row % 8},
            ).start()

        @pl.when(mine)
        def _():
            pltpu.make_async_copy(src, dst, c1_r.at[col]).start()

    @pl.when(row != 0)
    def _():
        remote(rp.at[own, :, 0:HALF], rp.at[own, :, 0:HALF], p1_s.at[0], p1_r, plane(0)).wait_recv()

    core_sends = [0]

    def core_panel(piece_rows, slot):
        src = rp.at[slot, piece_rows, 0:HALF]
        dst = po.at[slot, piece_rows]
        i = core_sends[0]
        core_sends[0] += 1
        send(src, dst, cp_s.at[i], cp_r.at[i], plane(core_row))

    whole = pl.ds(0, EB)
    send(rp.at[own], rp.at[own], br_s, br_r, to_ep)
    for direction in range(2):
        ring_send(rp, rs, rq, direction, 0, 0)
    core_panel(whole, own)
    other = (1 - ep) * 8 + col + 1
    remote(rp.at[other], rp.at[other], br_s, br_r, to_ep).wait_recv()
    for direction in range(2):
        ring_send(rp, rs, rq, direction, 0, 1)
    core_panel(whole, other)
    send(xr.at[own], xr.at[own], bx_s, bx_r, to_ep)
    for s in range(4):
        for k in range(2):
            for direction in range(2):
                ring_wait(rp, rs, rq, direction, s, k)
                if s < 3:
                    ring_send(rp, rs, rq, direction, s + 1, k)
                slot = eps[k] * 8 + ring_origin(direction, s + 1) + 1
                core_panel(whole if s < 3 else pl.ds(32 * direction, 32), slot)
    remote(xr.at[other], xr.at[other], bx_s, bx_r, to_ep).wait_recv()
    for direction in range(2):
        ring_send(xr, xs, xq, direction, 0, 1)

    q_own = row // 2
    mine8 = lambda k: pl.ds(k * 8 + 1, 8)

    def plane_send(i, q, dev_row, lo=0, n=8):
        piece = xc.at[q, pl.ds(core * 8 + 1 + lo, n)]
        send(piece, piece, c2_s.at[i], c2_r.at[i], plane(dev_row))

    def plane_wait(i, q, lo=0, n=8):
        piece = xc.at[q, pl.ds(core * 8 + 1 + lo, n)]
        remote(piece, piece, c2_s.at[i], c2_r.at[i], plane(core_row)).wait_recv()

    def core_send(i, q, lo=0, n=8):
        piece = xc.at[q, pl.ds(core * 8 + 1 + lo, n)]
        send(piece, piece, cc_s.at[i], cc_r.at[i], plane(core_row))

    def q_of(r):
        return r // 2

    q_x, q_up, q_down = q_of(x_row), q_of(yup_row), q_of(ydown_row)
    q_xup, q_xdown = q_of((x_row + 4) % 16), q_of((x_row + 12) % 16)
    q_opp, q_xopp = q_of((row + 8) % 16), q_of((x_row + 8) % 16)
    for z in range(8):
        piece = xc.at[q_own, core * 8 + z + 1]
        remote(piece, piece, c1_s.at[0], c1_r.at[z], plane(core_row)).wait_recv()
    plane_send(0, q_own, x_row)
    plane_send(1, q_own, yup_row)
    plane_send(2, q_own, ydown_row)
    core_send(0, q_own)

    arrivals = [(whole, own), (whole, other)]
    for s in range(4):
        for k in range(2):
            for direction in range(2):
                slot = eps[k] * 8 + ring_origin(direction, s + 1) + 1
                arrivals.append((whole if s < 3 else pl.ds(32 * direction, 32), slot))
    for i, (rows, slot) in enumerate(arrivals):
        remote(rp.at[slot, rows, 0:HALF], po.at[slot, rows], cp_s.at[i], cp_r.at[i], plane(core_row)).wait_recv()

    here = pl.ds(pl.multiple_of(core * HALF, HALF), HALF)
    there = pl.ds(pl.multiple_of((1 - core) * HALF, HALF), HALF)
    for e in range(NE):
        toep = rp[e + 1, :, HALF:]
        rows = slice(e * EB, (e + 1) * EB)
        pf[rows, here] = dot_nn(toep, rp[e : e + 2, :, :HALF].reshape(2 * EB, HALF)).astype(BF16)
        pf[rows, there] = dot_nn(toep, po[e : e + 2].reshape(2 * EB, HALF)).astype(BF16)
    for b in range(8):
        cut = slice(b * 128, (b + 1) * 128)
        pft[:, cut] = pf[cut, :].T
    smat[...] = dot_nn(pft[...], pf[...])
    di = lax.broadcasted_iota(jnp.int32, (PAN, PAN), 0)
    dj = lax.broadcasted_iota(jnp.int32, (PAN, PAN), 1)
    reg_diag = jnp.where(di == dj, reg_ref[:, :PAN], 0.0)
    smat[...] = smat[...] + reg_diag
    wmat[...] = jnp.zeros((PAN, PAN), F32)

    factor_step(smat, wmat, 0)

    def block_stage(s):
        for k in range(2):
            for direction in range(2):
                ring_wait(xr, xs, xq, direction, s, k)
                if s < 3:
                    ring_send(xr, xs, xq, direction, s + 1, k)

    block_stage(0)
    plane_wait(0, q_x)
    plane_send(3, q_x, yup_row)
    plane_send(4, q_x, ydown_row)
    core_send(1, q_x)
    plane_wait(1, q_down)
    plane_send(5, q_down, yup_row, 0, 4)
    core_send(2, q_down)
    plane_wait(2, q_up)
    plane_send(6, q_up, ydown_row, 4, 4)
    core_send(3, q_up)

    factor_step(smat, wmat, 1)
    block_stage(1)
    plane_wait(3, q_xdown)
    plane_send(7, q_xdown, yup_row, 0, 4)
    core_send(4, q_xdown)
    plane_wait(4, q_xup)
    plane_send(8, q_xup, ydown_row, 4, 4)
    core_send(5, q_xup)

    factor_step(smat, wmat, 2)
    block_stage(2)
    plane_wait(5, q_opp, 0, 4)
    plane_wait(6, q_opp, 4, 4)
    core_send(6, q_opp)
    plane_wait(7, q_xopp, 0, 4)
    plane_wait(8, q_xopp, 4, 4)
    core_send(7, q_xopp)

    factor_step(smat, wmat, 3)
    block_stage(3)
    for i, q in enumerate((q_own, q_x, q_down, q_up, q_xdown, q_xup, q_opp, q_xopp)):
        piece = xc.at[q, pl.ds((1 - core) * 8 + 1, 8)]
        remote(piece, piece, cc_s.at[i], cc_r.at[i], plane(core_row)).wait_recv()

    for e in range(0, NE, 2):
        pair = []
        for f in (e, e + 1):
            toep = rp[f + 1, :, HALF:]
            pair.append(dot_nn(toep, xr[f : f + 2].reshape(2 * EB, 1024)).astype(BF16))
            for q in range(8):
                fc_ref[f * EB : (f + 1) * EB, q * PB : (q + 1) * PB] = dot_nn(
                    toep, xc[q, f : f + 2].reshape(2 * EB, PB)
                ).astype(BF16)
        frt_ref[:, e * EB : (e + 2) * EB] = jnp.concatenate(pair, axis=0).T

    wh, wl = split2(wmat[...])
    wcat = jnp.concatenate([wh, wl, wh], axis=1)
    for b in range(2):
        cut = slice(b * PAN, (b + 1) * PAN)
        ar = dot_nn(frt_ref[cut, :], pf[...])
        if b == 0:
            ar = ar + jnp.where(row == 0, reg_diag, 0.0)
        ah, al = split2(ar)
        rr_ref[cut, :] = dot_nt(jnp.concatenate([ah, ah, al], axis=1), wcat)
        act = dot_nn(pft[...], fc_ref[:, cut])
        if b == 0:
            act = act + jnp.where(group == 0, reg_diag, 0.0)
        ah, al = split2(act)
        rct_ref[:, cut] = dot_nn(wcat, jnp.concatenate([ah, ah, al], axis=0))

    for copy in sends:
        copy.wait_send()
    for q in range(8):
        mine = jnp.logical_and(is_self, row // 2 == q)

        @pl.when(jnp.logical_not(mine))
        def _():
            remote(
                xr.at[own, :, q * PB : (q + 1) * PB], xc.at[q, own], c1_s.at[q], c1_r.at[col],
                {"ep": row // 8, "row": 2 * q + ep, "col": row % 8},
            ).wait_send()

    @pl.when(row == 0)
    def _():
        for t in range(1, 16):
            half = t % 2
            remote(
                xr.at[own, :, half * HALF : (half + 1) * HALF], rp.at[own, :, 0:HALF],
                p1_s.at[t - 1], p1_r, plane(t),
            ).wait_send()


def tile_kernel(frt_ref, fc_ref, rr_ref, rct_ref, reg_ref, out_ref, rcat):
    step = pl.program_id(0)
    rows_step = out_ref.shape[0]
    cols = out_ref.shape[1]
    row = lax.axis_index("row")
    group = lax.axis_index("ep") * 8 + lax.axis_index("col")

    @pl.when(step == 0)
    def _():
        rh, rl = split2(rct_ref[...])
        rcat[0:PAN] = rh
        rcat[PAN : 2 * PAN] = rl
        rcat[2 * PAN :] = rh

    base = row * 1024 + step * rows_step
    rr = rr_ref[...]
    ah, al = split2(rr)
    schur = dot_nn(jnp.concatenate([ah, ah, al], axis=1), rcat[...])
    tile = dot_nn(frt_ref[...], fc_ref[...])
    gr = base + lax.broadcasted_iota(jnp.int32, (rows_step, cols), 0)
    gc = group * 1024 + lax.broadcasted_iota(jnp.int32, (rows_step, cols), 1)
    reg = reg_ref[:, pl.ds(pl.multiple_of(group * 1024, 1024), 1024)]
    value = tile + jnp.where(gr == gc, reg, 0.0) - schur
    out_ref[...] = jnp.where(gr >= PAN, value, 0.0)

    @pl.when(group == 0)
    def _():
        pr = base + lax.broadcasted_iota(jnp.int32, (rows_step, PAN), 0)
        pc = lax.broadcasted_iota(jnp.int32, (rows_step, PAN), 1)
        out_ref[:, :PAN] = jnp.where(jnp.logical_and(pr < HALF, pc >= HALF), 0.0, rr)


def on_device(design, taps, tap_count, order, regular):
    vm = pl.BlockSpec(memory_space=pltpu.VMEM)
    dma = pltpu.SemaphoreType.DMA
    reg = regular.reshape(1, -1)
    frt, fc, rr, rct = pl.pallas_call(
        gather_kernel,
        out_shape=(
            jax.ShapeDtypeStruct((1024, 1024), BF16),
            jax.ShapeDtypeStruct((1024, 1024), BF16),
            jax.ShapeDtypeStruct((1024, PAN), F32),
            jax.ShapeDtypeStruct((PAN, 1024), F32),
        ),
        in_specs=[vm, pl.BlockSpec(memory_space=pltpu.SMEM), vm, vm, vm],
        out_specs=(vm, vm, vm, vm),
        scratch_shapes=[
            pltpu.VMEM((NE + 1, EB, 1024), BF16),
            pltpu.VMEM((8, NE + 1, EB, PB), BF16),
            pltpu.VMEM((NE + 1, EB, HALF + 128), BF16),
            pltpu.VMEM((NE + 1, EB, HALF), BF16),
            pltpu.VMEM((1024, PAN), BF16),
            pltpu.VMEM((PAN, 1024), BF16),
            pltpu.VMEM((PAN, PAN), F32),
            pltpu.VMEM((PAN, PAN), F32),
            dma, dma, dma, dma,
            dma((15,)), dma,
            dma((8,)), dma((8,)),
            dma((2, 4, 2)), dma((2, 4, 2)),
            dma((2, 4, 2)), dma((2, 4, 2)),
            dma((9,)), dma((9,)),
            dma((8,)), dma((8,)),
            dma((18,)), dma((18,)),
        ],
        compiler_params=pltpu.CompilerParams(
            collective_id=0, has_side_effects=True, vmem_limit_bytes=56 << 20
        ),
        name="gather",
    )(design, taps, tap_count.reshape(1, -1), order.reshape(1, -1), reg)
    rows_step = 128
    const = lambda shape: pl.BlockSpec(shape, lambda i: (0, 0), pipeline_mode=pl.Buffered(1))
    return pl.pallas_call(
        tile_kernel,
        grid=(1024 // rows_step,),
        out_shape=jax.ShapeDtypeStruct((1024, 1024), F32),
        in_specs=[
            pl.BlockSpec((rows_step, 1024), lambda i: (i, 0)),
            const((1024, 1024)),
            pl.BlockSpec((rows_step, PAN), lambda i: (i, 0)),
            const((PAN, 1024)),
            const((1, 16384)),
        ],
        out_specs=pl.BlockSpec((rows_step, 1024), lambda i: (i, 0)),
        scratch_shapes=[pltpu.VMEM((3 * PAN, 1024), BF16)],
        compiler_params=pltpu.CompilerParams(vmem_limit_bytes=40 << 20),
        name="tile",
    )(frt, fc, rr, rct, reg)


def solution(mesh):
    in_specs = (P(("ep", "col"), "row"), P(), P(("ep", "col")), P("row"), P())
    out_specs = P("row", ("ep", "col"))
    return jax.shard_map(
        on_device, mesh=mesh, in_specs=in_specs, out_specs=out_specs, check_vma=False
    )
```

profile of v0, /device:TPU:1, one launch (start us, length us, event | category | flops | bytes accessed | tf_op | source)
XLA Modules:
  0.0 95.9 jit_solution(3566788696136662613)
XLA Ops:
  0.0 80.3 %gather.1 = (bf16[1024,1024]{1,0:T(8,128)(2,1)}, bf16[1024,1024]{1,0:T(8,128)(2,1)}, f32[1024,512]{1,0:T(8,128)}, f32[512,1024]{1,0:T(8,128)}) custom-call(bf16[64,1024]{1,0:T(8,128)(2,1)} %design_ref.1, f32[64]{0:T(128)} %taps_ref.1, s32[1,64]{1,0:T(1,128)} %bitcast.6, s32[1,1024]{1,0:T(1,128)} %bitcast.5, f32[1,16384]{1,0:T(1,128)} %bitcast.3), custom_call_target="tpu_custom_call" | custom-call | tf_op jit(solution)/shard_map/gather/pallas_call | solution.py:462
  80.3 0.0 copy-start
  80.3 1.6 %copy-done = bf16[1024,1024]{1,0:T(8,128)(2,1)S(1)} copy-done((bf16[1024,1024]{1,0:T(8,128)(2,1)S(1)}, bf16[1024,1024]{1,0:T(8,128)(2,1)}, u32[]{:S(2)}) %copy-start) | copy-done | bytes 2097176
  81.9 0.0 copy-start.1
  81.9 1.6 %copy-done.1 = bf16[1024,1024]{1,0:T(8,128)(2,1)S(1)} copy-done((bf16[1024,1024]{1,0:T(8,128)(2,1)S(1)}, bf16[1024,1024]{1,0:T(8,128)(2,1)}, u32[]{:S(2)}) %copy-start.1) | copy-done | bytes 2097176
  83.4 0.0 copy-start.2
  83.5 1.6 %copy-done.2 = f32[1024,512]{1,0:T(8,128)S(1)} copy-done((f32[1024,512]{1,0:T(8,128)S(1)}, f32[1024,512]{1,0:T(8,128)}, u32[]{:S(2)}) %copy-start.2) | copy-done | bytes 2097176
  85.0 0.0 copy-start.3
  85.0 1.6 %copy-done.3 = f32[512,1024]{1,0:T(8,128)S(1)} copy-done((f32[512,1024]{1,0:T(8,128)S(1)}, f32[512,1024]{1,0:T(8,128)}, u32[]{:S(2)}) %copy-start.3) | copy-done | bytes 2097176
  86.6 0.0 copy-start.4
  86.6 0.8 copy-done.4
  87.5 8.5 %tile.1 = f32[1024,1024]{1,0:T(8,128)} custom-call(bf16[1024,1024]{1,0:T(8,128)(2,1)S(1)} %copy-done, bf16[1024,1024]{1,0:T(8,128)(2,1)S(1)} %copy-done.1, f32[1024,512]{1,0:T(8,128)S(1)} %copy-done.2, f32[512,1024]{1,0:T(8,128)S(1)} %copy-done.3, f32[1,16384]{1,0:T(1,128)S(1)} %bitcast.4), custom_call_target="tpu_custom_call" | custom-call | tf_op jit(solution)/shard_map/tile/pallas_call | solution.py:497
Async XLA Ops:
  80.3 1.6 %copy-start = (bf16[1024,1024]{1,0:T(8,128)(2,1)S(1)}, bf16[1024,1024]{1,0:T(8,128)(2,1)}, u32[]{:S(2)}) copy-start(bf16[1024,1024]{1,0:T(8,128)(2,1)} %get-tuple-element.9.frt_ref) | copy-start | bytes 6291460
  81.9 1.6 %copy-start.1 = (bf16[1024,1024]{1,0:T(8,128)(2,1)S(1)}, bf16[1024,1024]{1,0:T(8,128)(2,1)}, u32[]{:S(2)}) copy-start(bf16[1024,1024]{1,0:T(8,128)(2,1)} %get-tuple-element.10.fc_ref) | copy-start | bytes 6291460
  83.4 1.6 %copy-start.2 = (f32[1024,512]{1,0:T(8,128)S(1)}, f32[1024,512]{1,0:T(8,128)}, u32[]{:S(2)}) copy-start(f32[1024,512]{1,0:T(8,128)} %get-tuple-element.11.rr_ref) | copy-start | bytes 6291460
  85.0 1.6 %copy-start.3 = (f32[512,1024]{1,0:T(8,128)S(1)}, f32[512,1024]{1,0:T(8,128)}, u32[]{:S(2)}) copy-start(f32[512,1024]{1,0:T(8,128)} %get-tuple-element.12.rct_ref) | copy-start | bytes 6291460
  86.6 0.8 copy-start.4
where the time goes:
time: 96.2 us; the launch traced here: 95.9 us
  Pallas kernels  88.7 us (92%)
  local copies, waits for them, and re-layouts  7.19 us (7%)
    pallas_call x1, Pallas kernels, on_device(): pl.pallas_call(gather_kernel, out_shape=(jax.ShapeDtypeStruct((1024, 1024...  80.3 us
    pallas_call x1, Pallas kernels, on_device(): pl.pallas_call(tile_kernel, grid=(1024 // rows_step,), out_shape=jax.Shap...  8.45 us
    unnamed x10, local copies, waits for them, and re-layouts  7.19 us

commit v1 on v0

--- a/solution.py
+++ b/solution.py
@@ -16,6 +16,7 @@
 EB = 64
 NE = 16
 HALF = 256
+QR = EB + 16
 
 
 def dot_nn(a, b, precision=None):
@@ -43,7 +44,7 @@
     return jnp.broadcast_to(v[k : k + 1, :], (8, 128))
 
 
-def invert_factor(groups):
+def invert_factor(groups, hooks):
     sub = lax.broadcasted_iota(jnp.int32, (8, 128), 0)
     lane = lax.broadcasted_iota(jnp.int32, (8, 128), 1)
     a = list(groups)
@@ -91,13 +92,15 @@
                 gq = gq - d[k] * grow[k]
             a[q], g[q] = aq, gq
         g[p] = gp * lax.rsqrt(dvec)
+        if p in hooks:
+            hooks[p]()
     return g
 
 
-def factor_step(s, w, b):
+def factor_step(s, w, b, hooks={}):
     n = s.shape[0]
     lo, hi = 128 * b, 128 * b + 128
-    g = invert_factor([s[lo + 8 * q : lo + 8 * q + 8, lo:hi] for q in range(16)])
+    g = invert_factor([s[lo + 8 * q : lo + 8 * q + 8, lo:hi] for q in range(16)], hooks)
     for q in range(16):
         w[lo + 8 * q : lo + 8 * q + 8, lo:hi] = g[q]
     inv = w[lo:hi, lo:hi]
@@ -110,17 +113,32 @@
 
 
 def gather_kernel(
+    design_in, taps_in, count_in, order_in, reg_in,
+    frt_ref, fc_ref, rr_ref, rct_ref, regc_ref,
+    xr, xc, pq, band_ref, pf, pft, smat, wmat,
     design_ref, taps_ref, count_ref, order_ref, reg_ref,
-    frt_ref, fc_ref, rr_ref, rct_ref,
-    xr, xc, rp, po, pf, pft, smat, wmat,
-    bx_s, bx_r, br_s, br_r, p1_s, p1_r, c1_s, c1_r, xs, xq, rs, rq, c2_s, c2_r, cc_s, cc_r, cp_s, cp_r,
+    in_s, bx_s, bx_r, p1_s, p1_r, c1_s, c1_r, xs, xq, gr_s, gr_r, px_s, px_r, po_s, po_r, pc_s, pc_r,
+    c2_s, c2_r, cc_s, cc_r,
 ):
+    group = lax.axis_index("ep") * 8 + lax.axis_index("col")
+    loads = [
+        pltpu.make_async_copy(order_in, order_ref, in_s.at[0]),
+        pltpu.make_async_copy(design_in, design_ref, in_s.at[1]),
+        pltpu.make_async_copy(taps_in, taps_ref, in_s.at[2]),
+        pltpu.make_async_copy(count_in, count_ref, in_s.at[3]),
+        pltpu.make_async_copy(reg_in.at[:, pl.ds(0, PAN)], reg_ref, in_s.at[4]),
+        pltpu.make_async_copy(
+            reg_in.at[:, pl.ds(pl.multiple_of(group * 1024, 1024), 1024)], regc_ref, in_s.at[5]
+        ),
+    ]
+    for load in loads:
+        load.start()
     ep = lax.axis_index("ep")
     row = lax.axis_index("row")
     col = lax.axis_index("col")
     core = row % 2
     e_own = ep * 8 + col
-    group = e_own
+    line = row % 4
     up, down = (col + 1) % 8, (col + 7) % 8
     to_up = {"ep": ep, "row": row, "col": up}
     to_down = {"ep": ep, "row": row, "col": down}
@@ -133,8 +151,15 @@
     is_self = jnp.logical_and(row == group, core == ep)
 
     barrier = pltpu.get_barrier_semaphore()
-    for dev in (to_up, to_down, to_ep, plane(core_row), plane(x_row), plane(yup_row), plane(ydown_row)):
+    for dev in (plane(core_row), plane(x_row), plane(yup_row), plane(ydown_row)):
         pl.semaphore_signal(barrier, inc=1, device_id=dev, device_id_type=MESH)
+    mates = []
+    for dz, de in ((1, 0), (7, 0), (0, 1), (2, 0), (6, 0), (1, 1), (7, 1), (3, 0), (5, 0), (2, 1), (6, 1), (4, 0), (3, 1), (5, 1), (4, 1)):
+        mate_ep, mate_col = (ep + de) % 2, (col + dz) % 8
+        mates.append((mate_ep, mate_col))
+        pl.semaphore_signal(
+            barrier, inc=1, device_id={"ep": mate_ep, "row": row, "col": mate_col}, device_id_type=MESH
+        )
 
     @pl.when(row != 0)
     def _():
@@ -149,6 +174,8 @@
                 barrier, inc=1, device_id={"ep": core, "row": group, "col": z}, device_id_type=MESH
             )
 
+    for load in loads:
+        load.wait()
     local = order_ref[...] % PB
     kk = lax.broadcasted_iota(jnp.int32, (PB, 1024), 0)
     one_hot = jnp.where(kk == local, 1.0, 0.0).astype(BF16)
@@ -166,19 +193,20 @@
     for t in range(taps_ref.shape[0]):
         band = jnp.where(lag == t, taps_ref[t], band)
     band = jnp.where(lag.astype(F32) < counts, band, 0.0)
-    rp[own, :, HALF:] = band.astype(BF16)
+    band_ref[...] = band.astype(BF16)
+    pq[line, own, EB:, :] = band_ref[pl.ds(pl.multiple_of(16 * line, 16), 16), :]
     xr[0] = jnp.zeros(xr.shape[1:], BF16)
-    rp[0] = jnp.zeros(rp.shape[1:], BF16)
-    po[0] = jnp.zeros(po.shape[1:], BF16)
+    for u in range(4):
+        pq[u, 0] = jnp.zeros((QR, 128), BF16)
     for q in range(8):
         xc[q, 0] = jnp.zeros((EB, PB), BF16)
 
     @pl.when(row == 0)
     def _():
-        rp[own, :, :HALF] = xr[own, :, :HALF]
+        pq[0, own, :EB, :] = xr[own, :, :128]
 
     pl.semaphore_wait(
-        barrier, 7 + 8 + jnp.where(row == 0, 15, 0) - jnp.where(is_self, 1, 0)
+        barrier, 4 + 15 + 8 + jnp.where(row == 0, 15, 0) - jnp.where(is_self, 1, 0)
     )
 
     sends = []
@@ -196,9 +224,9 @@
     @pl.when(row == 0)
     def _():
         for t in range(1, 16):
-            half = t % 2
+            u = t % 4
             remote(
-                xr.at[own, :, half * HALF : (half + 1) * HALF], rp.at[own, :, 0:HALF],
+                xr.at[own, :, u * 128 : (u + 1) * 128], pq.at[u, own, 0:EB],
                 p1_s.at[t - 1], p1_r, plane(t),
             ).start()
 
@@ -239,63 +267,66 @@
         def _():
             pltpu.make_async_copy(src, dst, c1_r.at[col]).start()
 
+    send(xr.at[own], xr.at[own], bx_s, bx_r, to_ep)
+
     @pl.when(row != 0)
     def _():
-        remote(rp.at[own, :, 0:HALF], rp.at[own, :, 0:HALF], p1_s.at[0], p1_r, plane(0)).wait_recv()
-
-    core_sends = [0]
-
-    def core_panel(piece_rows, slot):
-        src = rp.at[slot, piece_rows, 0:HALF]
-        dst = po.at[slot, piece_rows]
-        i = core_sends[0]
-        core_sends[0] += 1
-        send(src, dst, cp_s.at[i], cp_r.at[i], plane(core_row))
-
-    whole = pl.ds(0, EB)
-    send(rp.at[own], rp.at[own], br_s, br_r, to_ep)
-    for direction in range(2):
-        ring_send(rp, rs, rq, direction, 0, 0)
-    core_panel(whole, own)
+        piece = pq.at[line, own, 0:EB]
+        remote(piece, piece, p1_s.at[0], p1_r, plane(0)).wait_recv()
+
+    x_line = (line + 2) % 4
+    back = (1, 0, 2, 4, 3, 6, 5, 8, 7, 10, 9, 11, 13, 12, 14)
+    slots = [own] + [a * 8 + z + 1 for a, z in mates]
+
+    def quarter_spread(i):
+        piece = pq.at[line, slots[i]]
+        send(piece, piece, px_s.at[i], px_r.at[i], plane(x_row))
+        send(piece, piece, po_s.at[i], po_r.at[i], plane(core_row))
+
+    def quarter_wait(i):
+        piece = pq.at[line, slots[i + 1]]
+        remote(piece, piece, gr_s.at[i], gr_r.at[back[i]], to_up).wait_recv()
+
+    def block_stage(s, k):
+        for direction in range(2):
+            ring_wait(xr, xs, xq, direction, s, k)
+            if s < 3:
+                ring_send(xr, xs, xq, direction, s + 1, k)
+
+    q_own = row // 2
+
+    def plane_send(i, q, dev_row, lo=0, n=8):
+        piece = xc.at[q, pl.ds(core * 8 + 1 + lo, n)]
+        send(piece, piece, c2_s.at[i], c2_r.at[i], plane(dev_row))
+
+    def plane_wait(i, q, lo=0, n=8):
+        piece = xc.at[q, pl.ds(core * 8 + 1 + lo, n)]
+        remote(piece, piece, c2_s.at[i], c2_r.at[i], plane(core_row)).wait_recv()
+
+    def core_send(i, q):
+        piece = xc.at[q, pl.ds(core * 8 + 1, 8)]
+        send(piece, piece, cc_s.at[i], cc_r.at[i], plane(core_row))
+
+    q_x, q_up, q_down = x_row // 2, yup_row // 2, ydown_row // 2
+    q_xup, q_xdown = ((x_row + 4) % 16) // 2, ((x_row + 12) % 16) // 2
+    q_opp, q_xopp = ((row + 8) % 16) // 2, ((x_row + 8) % 16) // 2
+
+    own_quarter = pq.at[line, own]
+    for i, (a, z) in enumerate(mates):
+        send(own_quarter, own_quarter, gr_s.at[i], gr_r.at[i], {"ep": a, "row": row, "col": z})
+    quarter_spread(0)
+    for i in range(15):
+        quarter_wait(i)
+        quarter_spread(i + 1)
+    for i in range(16):
+        piece = pq.at[x_line, slots[i]]
+        remote(piece, piece, px_s.at[i], px_r.at[i], plane(x_row)).wait_recv()
+        send(piece, piece, pc_s.at[i], pc_r.at[i], plane(core_row))
     other = (1 - ep) * 8 + col + 1
-    remote(rp.at[other], rp.at[other], br_s, br_r, to_ep).wait_recv()
-    for direction in range(2):
-        ring_send(rp, rs, rq, direction, 0, 1)
-    core_panel(whole, other)
-    send(xr.at[own], xr.at[own], bx_s, bx_r, to_ep)
-    for s in range(4):
-        for k in range(2):
-            for direction in range(2):
-                ring_wait(rp, rs, rq, direction, s, k)
-                if s < 3:
-                    ring_send(rp, rs, rq, direction, s + 1, k)
-                slot = eps[k] * 8 + ring_origin(direction, s + 1) + 1
-                core_panel(whole if s < 3 else pl.ds(32 * direction, 32), slot)
     remote(xr.at[other], xr.at[other], bx_s, bx_r, to_ep).wait_recv()
     for direction in range(2):
         ring_send(xr, xs, xq, direction, 0, 1)
-
-    q_own = row // 2
-    mine8 = lambda k: pl.ds(k * 8 + 1, 8)
-
-    def plane_send(i, q, dev_row, lo=0, n=8):
-        piece = xc.at[q, pl.ds(core * 8 + 1 + lo, n)]
-        send(piece, piece, c2_s.at[i], c2_r.at[i], plane(dev_row))
-
-    def plane_wait(i, q, lo=0, n=8):
-        piece = xc.at[q, pl.ds(core * 8 + 1 + lo, n)]
-        remote(piece, piece, c2_s.at[i], c2_r.at[i], plane(core_row)).wait_recv()
-
-    def core_send(i, q, lo=0, n=8):
-        piece = xc.at[q, pl.ds(core * 8 + 1 + lo, n)]
-        send(piece, piece, cc_s.at[i], cc_r.at[i], plane(core_row))
-
-    def q_of(r):
-        return r // 2
-
-    q_x, q_up, q_down = q_of(x_row), q_of(yup_row), q_of(ydown_row)
-    q_xup, q_xdown = q_of((x_row + 4) % 16), q_of((x_row + 12) % 16)
-    q_opp, q_xopp = q_of((row + 8) % 16), q_of((x_row + 8) % 16)
+    block_stage(0, 0)
     for z in range(8):
         piece = xc.at[q_own, core * 8 + z + 1]
         remote(piece, piece, c1_s.at[0], c1_r.at[z], plane(core_row)).wait_recv()
@@ -303,74 +334,76 @@
     plane_send(1, q_own, yup_row)
     plane_send(2, q_own, ydown_row)
     core_send(0, q_own)
-
-    arrivals = [(whole, own), (whole, other)]
-    for s in range(4):
-        for k in range(2):
-            for direction in range(2):
-                slot = eps[k] * 8 + ring_origin(direction, s + 1) + 1
-                arrivals.append((whole if s < 3 else pl.ds(32 * direction, 32), slot))
-    for i, (rows, slot) in enumerate(arrivals):
-        remote(rp.at[slot, rows, 0:HALF], po.at[slot, rows], cp_s.at[i], cp_r.at[i], plane(core_row)).wait_recv()
-
-    here = pl.ds(pl.multiple_of(core * HALF, HALF), HALF)
-    there = pl.ds(pl.multiple_of((1 - core) * HALF, HALF), HALF)
+    core_line = line + 1 - 2 * core
+    for i in range(16):
+        piece = pq.at[core_line, slots[i]]
+        remote(piece, piece, po_s.at[i], po_r.at[i], plane(core_row)).wait_recv()
+    core_line = (core_line + 2) % 4
+    for i in range(16):
+        piece = pq.at[core_line, slots[i]]
+        remote(piece, piece, pc_s.at[i], pc_r.at[i], plane(core_row)).wait_recv()
+
     for e in range(NE):
-        toep = rp[e + 1, :, HALF:]
-        rows = slice(e * EB, (e + 1) * EB)
-        pf[rows, here] = dot_nn(toep, rp[e : e + 2, :, :HALF].reshape(2 * EB, HALF)).astype(BF16)
-        pf[rows, there] = dot_nn(toep, po[e : e + 2].reshape(2 * EB, HALF)).astype(BF16)
+        toep = jnp.concatenate([pq[u, e + 1, EB:, :] for u in range(4)], axis=0)
+        panel = jnp.concatenate(
+            [jnp.concatenate([pq[u, e, :EB, :], pq[u, e + 1, :EB, :]], axis=0) for u in range(4)], axis=1
+        )
+        pf[e * EB : (e + 1) * EB, :] = dot_nn(toep, panel).astype(BF16)
     for b in range(8):
         cut = slice(b * 128, (b + 1) * 128)
         pft[:, cut] = pf[cut, :].T
     smat[...] = dot_nn(pft[...], pf[...])
     di = lax.broadcasted_iota(jnp.int32, (PAN, PAN), 0)
     dj = lax.broadcasted_iota(jnp.int32, (PAN, PAN), 1)
-    reg_diag = jnp.where(di == dj, reg_ref[:, :PAN], 0.0)
+    reg_diag = jnp.where(di == dj, reg_ref[...], 0.0)
     smat[...] = smat[...] + reg_diag
     wmat[...] = jnp.zeros((PAN, PAN), F32)
 
-    factor_step(smat, wmat, 0)
-
-    def block_stage(s):
-        for k in range(2):
-            for direction in range(2):
-                ring_wait(xr, xs, xq, direction, s, k)
-                if s < 3:
-                    ring_send(xr, xs, xq, direction, s + 1, k)
-
-    block_stage(0)
-    plane_wait(0, q_x)
-    plane_send(3, q_x, yup_row)
-    plane_send(4, q_x, ydown_row)
-    core_send(1, q_x)
-    plane_wait(1, q_down)
-    plane_send(5, q_down, yup_row, 0, 4)
-    core_send(2, q_down)
-    plane_wait(2, q_up)
-    plane_send(6, q_up, ydown_row, 4, 4)
-    core_send(3, q_up)
-
-    factor_step(smat, wmat, 1)
-    block_stage(1)
-    plane_wait(3, q_xdown)
-    plane_send(7, q_xdown, yup_row, 0, 4)
-    core_send(4, q_xdown)
-    plane_wait(4, q_xup)
-    plane_send(8, q_xup, ydown_row, 4, 4)
-    core_send(5, q_xup)
-
-    factor_step(smat, wmat, 2)
-    block_stage(2)
-    plane_wait(5, q_opp, 0, 4)
-    plane_wait(6, q_opp, 4, 4)
-    core_send(6, q_opp)
-    plane_wait(7, q_xopp, 0, 4)
-    plane_wait(8, q_xopp, 4, 4)
-    core_send(7, q_xopp)
-
+    def stage_a():
+        block_stage(0, 1)
+        plane_wait(0, q_x)
+        plane_send(3, q_x, yup_row)
+        plane_send(4, q_x, ydown_row)
+        core_send(1, q_x)
+        plane_wait(1, q_down)
+        plane_send(5, q_down, yup_row, 0, 4)
+        plane_wait(2, q_up)
+        plane_send(6, q_up, ydown_row, 4, 4)
+
+    def stage_b():
+        block_stage(1, 0)
+        core_send(2, q_down)
+        core_send(3, q_up)
+
+    def stage_c():
+        plane_wait(3, q_xdown)
+        plane_send(7, q_xdown, yup_row, 0, 4)
+        core_send(4, q_xdown)
+        plane_wait(4, q_xup)
+        plane_send(8, q_xup, ydown_row, 4, 4)
+        core_send(5, q_xup)
+
+    def stage_d():
+        block_stage(1, 1)
+
+    def stage_e():
+        block_stage(2, 0)
+
+    def stage_f():
+        block_stage(2, 1)
+        plane_wait(5, q_opp, 0, 4)
+        plane_wait(6, q_opp, 4, 4)
+        core_send(6, q_opp)
+        plane_wait(7, q_xopp, 0, 4)
+        plane_wait(8, q_xopp, 4, 4)
+        core_send(7, q_xopp)
+
+    factor_step(smat, wmat, 0, {11: stage_a})
+    factor_step(smat, wmat, 1, {3: stage_b, 11: stage_c, 15: stage_d})
+    factor_step(smat, wmat, 2, {7: stage_e, 15: stage_f})
     factor_step(smat, wmat, 3)
-    block_stage(3)
+    block_stage(3, 0)
+    block_stage(3, 1)
     for i, q in enumerate((q_own, q_x, q_down, q_up, q_xdown, q_xup, q_opp, q_xopp)):
         piece = xc.at[q, pl.ds((1 - core) * 8 + 1, 8)]
         remote(piece, piece, cc_s.at[i], cc_r.at[i], plane(core_row)).wait_recv()
@@ -378,7 +411,7 @@
     for e in range(0, NE, 2):
         pair = []
         for f in (e, e + 1):
-            toep = rp[f + 1, :, HALF:]
+            toep = jnp.concatenate([pq[u, f + 1, EB:, :] for u in range(4)], axis=0)
             pair.append(dot_nn(toep, xr[f : f + 2].reshape(2 * EB, 1024)).astype(BF16))
             for q in range(8):
                 fc_ref[f * EB : (f + 1) * EB, q * PB : (q + 1) * PB] = dot_nn(
@@ -416,9 +449,9 @@
     @pl.when(row == 0)
     def _():
         for t in range(1, 16):
-            half = t % 2
+            u = t % 4
             remote(
-                xr.at[own, :, half * HALF : (half + 1) * HALF], rp.at[own, :, 0:HALF],
+                xr.at[own, :, u * 128 : (u + 1) * 128], pq.at[u, own, 0:EB],
                 p1_s.at[t - 1], p1_r, plane(t),
             ).wait_send()
 
@@ -438,13 +471,14 @@
         rcat[2 * PAN :] = rh
 
     base = row * 1024 + step * rows_step
-    rr = rr_ref[...]
+    here = pl.ds(pl.multiple_of(step * rows_step, rows_step), rows_step)
+    rr = rr_ref[here, :]
     ah, al = split2(rr)
     schur = dot_nn(jnp.concatenate([ah, ah, al], axis=1), rcat[...])
-    tile = dot_nn(frt_ref[...], fc_ref[...])
+    tile = dot_nn(frt_ref[here, :], fc_ref[...])
     gr = base + lax.broadcasted_iota(jnp.int32, (rows_step, cols), 0)
     gc = group * 1024 + lax.broadcasted_iota(jnp.int32, (rows_step, cols), 1)
-    reg = reg_ref[:, pl.ds(pl.multiple_of(group * 1024, 1024), 1024)]
+    reg = reg_ref[...]
     value = tile + jnp.where(gr == gc, reg, 0.0) - schur
     out_ref[...] = jnp.where(gr >= PAN, value, 0.0)
 
@@ -459,57 +493,61 @@
     vm = pl.BlockSpec(memory_space=pltpu.VMEM)
     dma = pltpu.SemaphoreType.DMA
     reg = regular.reshape(1, -1)
-    frt, fc, rr, rct = pl.pallas_call(
+    frt, fc, rr, rct, regc = pl.pallas_call(
         gather_kernel,
         out_shape=(
-            jax.ShapeDtypeStruct((1024, 1024), BF16),
-            jax.ShapeDtypeStruct((1024, 1024), BF16),
-            jax.ShapeDtypeStruct((1024, PAN), F32),
-            jax.ShapeDtypeStruct((PAN, 1024), F32),
+            pltpu.VMEM((1024, 1024), BF16),
+            pltpu.VMEM((1024, 1024), BF16),
+            pltpu.VMEM((1024, PAN), F32),
+            pltpu.VMEM((PAN, 1024), F32),
+            pltpu.VMEM((1, 1024), F32),
         ),
-        in_specs=[vm, pl.BlockSpec(memory_space=pltpu.SMEM), vm, vm, vm],
-        out_specs=(vm, vm, vm, vm),
+        in_specs=[pl.BlockSpec(memory_space=pltpu.HBM)] * 5,
+        out_specs=(vm, vm, vm, vm, vm),
         scratch_shapes=[
             pltpu.VMEM((NE + 1, EB, 1024), BF16),
             pltpu.VMEM((8, NE + 1, EB, PB), BF16),
-            pltpu.VMEM((NE + 1, EB, HALF + 128), BF16),
-            pltpu.VMEM((NE + 1, EB, HALF), BF16),
+            pltpu.VMEM((4, NE + 1, QR, 128), BF16),
+            pltpu.VMEM((EB, 128), BF16),
             pltpu.VMEM((1024, PAN), BF16),
             pltpu.VMEM((PAN, 1024), BF16),
             pltpu.VMEM((PAN, PAN), F32),
             pltpu.VMEM((PAN, PAN), F32),
-            dma, dma, dma, dma,
+            pltpu.VMEM((EB, 1024), BF16),
+            pltpu.SMEM((64,), F32),
+            pltpu.VMEM((1, EB), jnp.int32),
+            pltpu.VMEM((1, 1024), jnp.int32),
+            pltpu.VMEM((1, PAN), F32),
+            dma((6,)),
+            dma, dma,
             dma((15,)), dma,
             dma((8,)), dma((8,)),
             dma((2, 4, 2)), dma((2, 4, 2)),
-            dma((2, 4, 2)), dma((2, 4, 2)),
+            dma((15,)), dma((15,)),
+            dma((16,)), dma((16,)),
+            dma((16,)), dma((16,)),
+            dma((16,)), dma((16,)),
             dma((9,)), dma((9,)),
             dma((8,)), dma((8,)),
-            dma((18,)), dma((18,)),
         ],
         compiler_params=pltpu.CompilerParams(
-            collective_id=0, has_side_effects=True, vmem_limit_bytes=56 << 20
+            collective_id=0, has_side_effects=True, vmem_limit_bytes=58450000
         ),
         name="gather",
     )(design, taps, tap_count.reshape(1, -1), order.reshape(1, -1), reg)
     rows_step = 128
-    const = lambda shape: pl.BlockSpec(shape, lambda i: (0, 0), pipeline_mode=pl.Buffered(1))
     return pl.pallas_call(
         tile_kernel,
         grid=(1024 // rows_step,),
         out_shape=jax.ShapeDtypeStruct((1024, 1024), F32),
         in_specs=[
-            pl.BlockSpec((rows_step, 1024), lambda i: (i, 0)),
-            const((1024, 1024)),
-            pl.BlockSpec((rows_step, PAN), lambda i: (i, 0)),
-            const((PAN, 1024)),
-            const((1, 16384)),
+            vm, vm, vm, vm, vm,
         ],
         out_specs=pl.BlockSpec((rows_step, 1024), lambda i: (i, 0)),
         scratch_shapes=[pltpu.VMEM((3 * PAN, 1024), BF16)],
-        compiler_params=pltpu.CompilerParams(vmem_limit_bytes=40 << 20),
+        compiler_params=pltpu.CompilerParams(vmem_limit_bytes=36 << 20),
         name="tile",
-    )(frt, fc, rr, rct, reg)
+    )(frt, fc, rr, rct, regc)
 
 
 def solution(mesh):

time: 96.2 us -> 80.9 us (0.84)
  Pallas kernels: 88.7 us -> 80.8 us
  local copies, waits for them, and re-layouts: 7.19 us -> 0 us
    pallas_call x1, Pallas kernels: 80.3 us -> 72.2 us  [on_device(): pl.pallas_call(gather_kernel, out_shape=(pltpu.VMEM((1024, 1024), BF16),...]
    unnamed x10 -> x0, local copies, waits for them, and re-layouts: 7.19 us -> none
where the time goes in v1:
time: 80.9 us; the launch traced here: 80.8 us
  Pallas kernels  80.8 us (100%)
    pallas_call x1, Pallas kernels, on_device(): pl.pallas_call(gather_kernel, out_shape=(pltpu.VMEM((1024, 1024), BF16),...  72.2 us
    pallas_call x1, Pallas kernels, on_device(): pl.pallas_call(tile_kernel, grid=(1024 // rows_step,), out_shape=jax.Shap...  8.58 us

profile of v1, /device:TPU:1, one launch (start us, length us, event | category | flops | bytes accessed | tf_op | source)
XLA Modules:
  0.0 80.8 jit_solution(9065620938220519392)
XLA Ops:
  0.0 72.2 %gather.1 = (bf16[1024,1024]{1,0:T(8,128)(2,1)S(1)}, bf16[1024,1024]{1,0:T(8,128)(2,1)S(1)}, f32[1024,512]{1,0:T(8,128)S(1)}, f32[512,1024]{1,0:T(8,128)S(1)}, f32[1,1024]{1,0:T(1,128)S(1)}) custom-call(bf16[64,1024]{1,0:T(8,128)(2,1)} %design_in.1, f32[64]{0:T(128)} %taps_in.1, s32[1,64]{1,0:T(1,128)} %bitcast.5, s32[1,1024]{1,0:T(1,128)} %bitcast.4, ...), custom_call_target="tpu_custom_call" | custom-call | tf_op jit(solution)/shard_map/gather/pallas_call | solution.py:496
  72.2 8.6 %tile.1 = f32[1024,1024]{1,0:T(8,128)} custom-call(bf16[1024,1024]{1,0:T(8,128)(2,1)S(1)} %get-tuple-element.10.frt_ref, bf16[1024,1024]{1,0:T(8,128)(2,1)S(1)} %get-tuple-element.11.fc_ref, f32[1024,512]{1,0:T(8,128)S(1)} %get-tuple-element.12.rr_ref, f32[512,1024]{1,0:T(8,128)S(1)} %get-tuple-element.13.rct_ref, f32[1,1024]{1,0:T(1,128)S(1)} %get-tuple-element.14.reg_ref), custom_call_target="tpu_custom_call" | custom-call | tf_op jit(solution)/shard_map/tile/pallas_call | solution.py:539

commit v2 on v1

--- a/solution.py
+++ b/solution.py
@@ -40,67 +40,60 @@
     return jnp.broadcast_to(v[:, j : j + 1], (8, 128))
 
 
-def row_bcast(v, k):
-    return jnp.broadcast_to(v[k : k + 1, :], (8, 128))
-
-
-def invert_factor(groups, hooks):
+def reciprocal(x):
+    r = pl.reciprocal(x, approx=True)
+    r = r * (2.0 - x * r)
+    return r * (2.0 - x * r)
+
+
+def invert_factor(groups, spread, hooks):
     sub = lax.broadcasted_iota(jnp.int32, (8, 128), 0)
     lane = lax.broadcasted_iota(jnp.int32, (8, 128), 1)
     a = list(groups)
-    g = [jnp.where(lane == sub + 8 * q, 1.0, 0.0).astype(F32) for q in range(16)]
+    out = [None] * 16
     for p in range(16):
+        base = (p % 2) * 72
         v = a[p]
         c = [lane_bcast(v, 8 * p + k) for k in range(8)]
+        here = (lane >= 8 * p) & (lane < 8 * p + 8)
+        m = jnp.where(here, jnp.where(lane - 8 * p == sub, 1.0, 0.0), v)
+        for k in range(8):
+            spread[base + 8 * k : base + 8 * k + 8, :] = c[k]
+        spread[base + 64 : base + 72, :] = m
         s = [[None] * 8 for _ in range(8)]
         for k in range(8):
             for i in range(k, 8):
-                s[i][k] = row_bcast(c[k], i)
-        rinv = [None] * 8
-        lcol = [None] * 8
-        dvec = None
-        gp = g[p]
+                s[i][k] = spread[pl.ds(base + 8 * k + i, 8, stride=0), :]
+        rows = [spread[pl.ds(base + 64 + k, 8, stride=0), :] for k in range(8)]
+        later = range(p + 1, 16)
+        d = {q: [lane_bcast(a[q], 8 * p + k) for k in range(8)] for q in later}
+        for q in later:
+            a[q] = jnp.where(here, 0.0, a[q])
         for k in range(8):
-            r = 1.0 / s[k][k]
-            rinv[k] = r
+            r = reciprocal(s[k][k])
             for i in range(k + 1, 8):
-                m = s[i][k] * r
+                w = s[i][k] * r
                 for j in range(k + 1, i + 1):
-                    s[i][j] = s[i][j] - m * s[j][k]
-            if k < 7:
-                lcol[k] = jnp.where(sub > k, c[k] * r, 0.0)
-                for m in range(k + 1, 8):
-                    c[m] = c[m] - lcol[k] * s[m][k]
-            dvec = s[k][k] if dvec is None else jnp.where(sub == k, s[k][k], dvec)
-        vrow = [None] * 8
-        grow = [None] * 8
-        for k in range(8):
-            vrow[k] = row_bcast(v, k)
-            grow[k] = row_bcast(gp, k)
-            if k < 7:
-                v = v - lcol[k] * vrow[k]
-                gp = gp - lcol[k] * grow[k]
-        for q in range(p + 1, 16):
-            d = [lane_bcast(a[q], 8 * p + k) for k in range(8)]
-            for k in range(8):
-                d[k] = d[k] * rinv[k]
-                for m in range(k + 1, 8):
-                    d[m] = d[m] - d[k] * s[m][k]
-            aq, gq = a[q], g[q]
-            for k in range(8):
-                aq = aq - d[k] * vrow[k]
-                gq = gq - d[k] * grow[k]
-            a[q], g[q] = aq, gq
-        g[p] = gp * lax.rsqrt(dvec)
+                    s[i][j] = s[i][j] - w * s[j][k]
+                rows[i] = rows[i] - w * rows[k]
+            for q in later:
+                w = d[q][k] * r
+                for i in range(k + 1, 8):
+                    d[q][i] = d[q][i] - w * s[i][k]
+                a[q] = a[q] - w * rows[k]
+        done = rows[0] * lax.rsqrt(s[0][0])
+        for k in range(1, 8):
+            done = jnp.where(sub == k, rows[k] * lax.rsqrt(s[k][k]), done)
+        out[p] = jnp.where(lane < 8 * p + 8, done, 0.0)
         if p in hooks:
             hooks[p]()
-    return g
-
-
-def factor_step(s, w, b, hooks={}):
+    return out
+
+
+def factor_step(s, w, spread, b, hooks={}):
     n = s.shape[0]
     lo, hi = 128 * b, 128 * b + 128
-    g = invert_factor([s[lo + 8 * q : lo + 8 * q + 8, lo:hi] for q in range(16)], hooks)
+    g = invert_factor([s[lo + 8 * q : lo + 8 * q + 8, lo:hi] for q in range(16)], spread, hooks)
     for q in range(16):
         w[lo + 8 * q : lo + 8 * q + 8, lo:hi] = g[q]
     inv = w[lo:hi, lo:hi]
@@ -115,7 +108,7 @@
 def gather_kernel(
     design_in, taps_in, count_in, order_in, reg_in,
     frt_ref, fc_ref, rr_ref, rct_ref, regc_ref,
-    xr, xc, pq, band_ref, pf, pft, smat, wmat,
+    xr, xc, pq, band_ref, pf, pft, smat, wmat, spread,
     design_ref, taps_ref, count_ref, order_ref, reg_ref,
     in_s, bx_s, bx_r, p1_s, p1_r, c1_s, c1_r, xs, xq, gr_s, gr_r, px_s, px_r, po_s, po_r, pc_s, pc_r,
     c2_s, c2_r, cc_s, cc_r,
@@ -318,21 +311,21 @@
     for i in range(15):
         quarter_wait(i)
         quarter_spread(i + 1)
+    block_stage(0, 0)
+    other = (1 - ep) * 8 + col + 1
+    remote(xr.at[other], xr.at[other], bx_s, bx_r, to_ep).wait_recv()
+    for direction in range(2):
+        ring_send(xr, xs, xq, direction, 0, 1)
+    for z in range(8):
+        piece = xc.at[q_own, core * 8 + z + 1]
+        remote(piece, piece, c1_s.at[0], c1_r.at[z], plane(core_row)).wait_recv()
+    plane_send(1, q_own, yup_row)
+    plane_send(2, q_own, ydown_row)
+    plane_send(0, q_own, x_row)
     for i in range(16):
         piece = pq.at[x_line, slots[i]]
         remote(piece, piece, px_s.at[i], px_r.at[i], plane(x_row)).wait_recv()
         send(piece, piece, pc_s.at[i], pc_r.at[i], plane(core_row))
-    other = (1 - ep) * 8 + col + 1
-    remote(xr.at[other], xr.at[other], bx_s, bx_r, to_ep).wait_recv()
-    for direction in range(2):
-        ring_send(xr, xs, xq, direction, 0, 1)
-    block_stage(0, 0)
-    for z in range(8):
-        piece = xc.at[q_own, core * 8 + z + 1]
-        remote(piece, piece, c1_s.at[0], c1_r.at[z], plane(core_row)).wait_recv()
-    plane_send(0, q_own, x_row)
-    plane_send(1, q_own, yup_row)
-    plane_send(2, q_own, ydown_row)
     core_send(0, q_own)
     core_line = line + 1 - 2 * core
     for i in range(16):
@@ -343,12 +336,21 @@
         piece = pq.at[core_line, slots[i]]
         remote(piece, piece, pc_s.at[i], pc_r.at[i], plane(core_row)).wait_recv()
 
-    for e in range(NE):
-        toep = jnp.concatenate([pq[u, e + 1, EB:, :] for u in range(4)], axis=0)
+    block_stage(1, 0)
+
+    zero = jnp.zeros((EB, EB), BF16)
+
+    def toeplitz_pair(e):
+        first, second = (jnp.concatenate([pq[u, f + 1, EB:, :] for u in range(4)], axis=0) for f in (e, e + 1))
+        return jnp.concatenate(
+            [jnp.concatenate([first, zero], axis=1), jnp.concatenate([zero, second], axis=1)], axis=0
+        )
+
+    for e in range(0, NE, 2):
         panel = jnp.concatenate(
-            [jnp.concatenate([pq[u, e, :EB, :], pq[u, e + 1, :EB, :]], axis=0) for u in range(4)], axis=1
+            [jnp.concatenate([pq[u, f, :EB, :] for f in (e, e + 1, e + 2)], axis=0) for u in range(4)], axis=1
         )
-        pf[e * EB : (e + 1) * EB, :] = dot_nn(toep, panel).astype(BF16)
+        pf[e * EB : (e + 2) * EB, :] = dot_nn(toeplitz_pair(e), panel).astype(BF16)
     for b in range(8):
         cut = slice(b * 128, (b + 1) * 128)
         pft[:, cut] = pf[cut, :].T
@@ -360,20 +362,19 @@
     wmat[...] = jnp.zeros((PAN, PAN), F32)
 
     def stage_a():
-        block_stage(0, 1)
+        plane_wait(1, q_down)
+        plane_send(5, q_down, yup_row, 0, 4)
+        plane_wait(2, q_up)
+        plane_send(6, q_up, ydown_row, 4, 4)
         plane_wait(0, q_x)
         plane_send(3, q_x, yup_row)
         plane_send(4, q_x, ydown_row)
         core_send(1, q_x)
-        plane_wait(1, q_down)
-        plane_send(5, q_down, yup_row, 0, 4)
-        plane_wait(2, q_up)
-        plane_send(6, q_up, ydown_row, 4, 4)
-
-    def stage_b():
-        block_stage(1, 0)
         core_send(2, q_down)
         core_send(3, q_up)
+
+    def stage_b():
+        block_stage(2, 0)
 
     def stage_c():
         plane_wait(3, q_xdown)
@@ -387,10 +388,9 @@
         block_stage(1, 1)
 
     def stage_e():
-        block_stage(2, 0)
+        block_stage(2, 1)
 
     def stage_f():
-        block_stage(2, 1)
         plane_wait(5, q_opp, 0, 4)
         plane_wait(6, q_opp, 4, 4)
         core_send(6, q_opp)
@@ -398,10 +398,11 @@
         plane_wait(8, q_xopp, 4, 4)
         core_send(7, q_xopp)
 
-    factor_step(smat, wmat, 0, {11: stage_a})
-    factor_step(smat, wmat, 1, {3: stage_b, 11: stage_c, 15: stage_d})
-    factor_step(smat, wmat, 2, {7: stage_e, 15: stage_f})
-    factor_step(smat, wmat, 3)
+    block_stage(0, 1)
+    factor_step(smat, wmat, spread, 0, {7: stage_a, 15: stage_b})
+    factor_step(smat, wmat, spread, 1, {3: stage_d, 9: stage_c})
+    factor_step(smat, wmat, spread, 2, {3: stage_e, 15: stage_f})
+    factor_step(smat, wmat, spread, 3)
     block_stage(3, 0)
     block_stage(3, 1)
     for i, q in enumerate((q_own, q_x, q_down, q_up, q_xdown, q_xup, q_opp, q_xopp)):
@@ -409,30 +410,39 @@
         remote(piece, piece, cc_s.at[i], cc_r.at[i], plane(core_row)).wait_recv()
 
     for e in range(0, NE, 2):
-        pair = []
-        for f in (e, e + 1):
-            toep = jnp.concatenate([pq[u, f + 1, EB:, :] for u in range(4)], axis=0)
-            pair.append(dot_nn(toep, xr[f : f + 2].reshape(2 * EB, 1024)).astype(BF16))
-            for q in range(8):
-                fc_ref[f * EB : (f + 1) * EB, q * PB : (q + 1) * PB] = dot_nn(
-                    toep, xc[q, f : f + 2].reshape(2 * EB, PB)
-                ).astype(BF16)
-        frt_ref[:, e * EB : (e + 2) * EB] = jnp.concatenate(pair, axis=0).T
+        toep = toeplitz_pair(e)
+        cut = slice(e * EB, (e + 2) * EB)
+        frt_ref[:, cut] = dot_nn(toep, xr[e : e + 3].reshape(3 * EB, 1024)).astype(BF16).T
+        columns = jnp.concatenate([xc[q, e : e + 3].reshape(3 * EB, PB) for q in range(8)], axis=1)
+        fc_ref[cut, :] = dot_nn(toep, columns).astype(BF16)
 
     wh, wl = split2(wmat[...])
-    wcat = jnp.concatenate([wh, wl, wh], axis=1)
+
+    def solve_weights(half):
+        rows, depth = slice(half * HALF, (half + 1) * HALF), (half + 1) * HALF
+        return jnp.concatenate([wh[rows, :depth], wl[rows, :depth], wh[rows, :depth]], axis=1)
+
+    weights = [solve_weights(half) for half in range(2)]
     for b in range(2):
         cut = slice(b * PAN, (b + 1) * PAN)
         ar = dot_nn(frt_ref[cut, :], pf[...])
         if b == 0:
             ar = ar + jnp.where(row == 0, reg_diag, 0.0)
         ah, al = split2(ar)
-        rr_ref[cut, :] = dot_nt(jnp.concatenate([ah, ah, al], axis=1), wcat)
+        for half in range(2):
+            depth = (half + 1) * HALF
+            rr_ref[cut, half * HALF : depth] = dot_nt(
+                jnp.concatenate([ah[:, :depth], ah[:, :depth], al[:, :depth]], axis=1), weights[half]
+            )
         act = dot_nn(pft[...], fc_ref[:, cut])
         if b == 0:
             act = act + jnp.where(group == 0, reg_diag, 0.0)
         ah, al = split2(act)
-        rct_ref[:, cut] = dot_nn(wcat, jnp.concatenate([ah, ah, al], axis=0))
+        for half in range(2):
+            depth = (half + 1) * HALF
+            rct_ref[half * HALF : depth, cut] = dot_nn(
+                weights[half], jnp.concatenate([ah[:depth], ah[:depth], al[:depth]], axis=0)
+            )
 
     for copy in sends:
         copy.wait_send()
@@ -513,6 +523,7 @@
             pltpu.VMEM((PAN, 1024), BF16),
             pltpu.VMEM((PAN, PAN), F32),
             pltpu.VMEM((PAN, PAN), F32),
+            pltpu.VMEM((144, 128), F32),
             pltpu.VMEM((EB, 1024), BF16),
             pltpu.SMEM((64,), F32),
             pltpu.VMEM((1, EB), jnp.int32),
@@ -535,7 +546,7 @@
         ),
         name="gather",
     )(design, taps, tap_count.reshape(1, -1), order.reshape(1, -1), reg)
-    rows_step = 128
+    rows_step = 256
     return pl.pallas_call(
         tile_kernel,
         grid=(1024 // rows_step,),

time: 80.9 us -> 75.8 us (0.937)
  Pallas kernels: 80.8 us -> 75.6 us
    pallas_call x1, Pallas kernels: 72.2 us -> 67.8 us  [on_device(): pl.pallas_call(gather_kernel, out_shape=(pltpu.VMEM((1024, 1024), BF16),...]
where the time goes in v2:
time: 75.8 us; the launch traced here: 75.6 us
  Pallas kernels  75.6 us (100%)
    pallas_call x1, Pallas kernels, on_device(): pl.pallas_call(gather_kernel, out_shape=(pltpu.VMEM((1024, 1024), BF16),...  67.8 us
    pallas_call x1, Pallas kernels, on_device(): pl.pallas_call(tile_kernel, grid=(1024 // rows_step,), out_shape=jax.Shap...  7.87 us

profile of v2, /device:TPU:1, one launch (start us, length us, event | category | flops | bytes accessed | tf_op | source)
XLA Modules:
  0.0 75.6 jit_solution(472741817755342212)
XLA Ops:
  0.0 67.8 %gather.1 = (bf16[1024,1024]{1,0:T(8,128)(2,1)S(1)}, bf16[1024,1024]{1,0:T(8,128)(2,1)S(1)}, f32[1024,512]{1,0:T(8,128)S(1)}, f32[512,1024]{1,0:T(8,128)S(1)}, f32[1,1024]{1,0:T(1,128)S(1)}) custom-call(bf16[64,1024]{1,0:T(8,128)(2,1)} %design_in.1, f32[64]{0:T(128)} %taps_in.1, s32[1,64]{1,0:T(1,128)} %bitcast.5, s32[1,1024]{1,0:T(1,128)} %bitcast.4, ...), custom_call_target="tpu_custom_call" | custom-call | tf_op jit(solution)/shard_map/gather/pallas_call | solution.py:506
  67.8 7.9 %tile.1 = f32[1024,1024]{1,0:T(8,128)} custom-call(bf16[1024,1024]{1,0:T(8,128)(2,1)S(1)} %get-tuple-element.10.frt_ref, bf16[1024,1024]{1,0:T(8,128)(2,1)S(1)} %get-tuple-element.11.fc_ref, f32[1024,512]{1,0:T(8,128)S(1)} %get-tuple-element.12.rr_ref, f32[512,1024]{1,0:T(8,128)S(1)} %get-tuple-element.13.rct_ref, f32[1,1024]{1,0:T(1,128)S(1)} %get-tuple-element.14.reg_ref), custom_call_target="tpu_custom_call" | custom-call | tf_op jit(solution)/shard_map/tile/pallas_call | solution.py:550

commit v3 on v2

--- a/solution.py
+++ b/solution.py
@@ -244,6 +244,52 @@
 
     for direction in range(2):
         ring_send(xr, xs, xq, direction, 0, 0)
+    @pl.when(row != 0)
+    def _():
+        piece = pq.at[line, own, 0:EB]
+        remote(piece, piece, p1_s.at[0], p1_r, plane(0)).wait_recv()
+
+    x_line = (line + 2) % 4
+    back = (1, 0, 2, 4, 3, 6, 5, 8, 7, 10, 9, 11, 13, 12, 14)
+    slots = [own] + [a * 8 + z + 1 for a, z in mates]
+
+    def quarter_spread(i):
+        piece = pq.at[line, slots[i]]
+        send(piece, piece, px_s.at[i], px_r.at[i], plane(x_row))
+        send(piece, piece, po_s.at[i], po_r.at[i], plane(core_row))
+
+    def quarter_wait(i):
+        piece = pq.at[line, slots[i + 1]]
+        remote(piece, piece, gr_s.at[i], gr_r.at[back[i]], to_up).wait_recv()
+
+    def block_stage(s, k):
+        for direction in range(2):
+            ring_wait(xr, xs, xq, direction, s, k)
+            if s < 3:
+                ring_send(xr, xs, xq, direction, s + 1, k)
+
+    q_own = row // 2
+
+    def plane_send(i, q, dev_row, lo=0, n=8):
+        piece = xc.at[q, pl.ds(core * 8 + 1 + lo, n)]
+        send(piece, piece, c2_s.at[i], c2_r.at[i], plane(dev_row))
+
+    def plane_wait(i, q, lo=0, n=8):
+        piece = xc.at[q, pl.ds(core * 8 + 1 + lo, n)]
+        remote(piece, piece, c2_s.at[i], c2_r.at[i], plane(core_row)).wait_recv()
+
+    def core_send(i, q):
+        piece = xc.at[q, pl.ds(core * 8 + 1, 8)]
+        send(piece, piece, cc_s.at[i], cc_r.at[i], plane(core_row))
+
+    q_x, q_up, q_down = x_row // 2, yup_row // 2, ydown_row // 2
+    q_xup, q_xdown = ((x_row + 4) % 16) // 2, ((x_row + 12) % 16) // 2
+    q_opp, q_xopp = ((row + 8) % 16) // 2, ((x_row + 8) % 16) // 2
+
+    own_quarter = pq.at[line, own]
+    for i, (a, z) in enumerate(mates):
+        send(own_quarter, own_quarter, gr_s.at[i], gr_r.at[i], {"ep": a, "row": row, "col": z})
+    quarter_spread(0)
     for q in range(8):
         src = xr.at[own, :, q * PB : (q + 1) * PB]
         dst = xc.at[q, own]
@@ -261,53 +307,6 @@
             pltpu.make_async_copy(src, dst, c1_r.at[col]).start()
 
     send(xr.at[own], xr.at[own], bx_s, bx_r, to_ep)
-
-    @pl.when(row != 0)
-    def _():
-        piece = pq.at[line, own, 0:EB]
-        remote(piece, piece, p1_s.at[0], p1_r, plane(0)).wait_recv()
-
-    x_line = (line + 2) % 4
-    back = (1, 0, 2, 4, 3, 6, 5, 8, 7, 10, 9, 11, 13, 12, 14)
-    slots = [own] + [a * 8 + z + 1 for a, z in mates]
-
-    def quarter_spread(i):
-        piece = pq.at[line, slots[i]]
-        send(piece, piece, px_s.at[i], px_r.at[i], plane(x_row))
-        send(piece, piece, po_s.at[i], po_r.at[i], plane(core_row))
-
-    def quarter_wait(i):
-        piece = pq.at[line, slots[i + 1]]
-        remote(piece, piece, gr_s.at[i], gr_r.at[back[i]], to_up).wait_recv()
-
-    def block_stage(s, k):
-        for direction in range(2):
-            ring_wait(xr, xs, xq, direction, s, k)
-            if s < 3:
-                ring_send(xr, xs, xq, direction, s + 1, k)
-
-    q_own = row // 2
-
-    def plane_send(i, q, dev_row, lo=0, n=8):
-        piece = xc.at[q, pl.ds(core * 8 + 1 + lo, n)]
-        send(piece, piece, c2_s.at[i], c2_r.at[i], plane(dev_row))
-
-    def plane_wait(i, q, lo=0, n=8):
-        piece = xc.at[q, pl.ds(core * 8 + 1 + lo, n)]
-        remote(piece, piece, c2_s.at[i], c2_r.at[i], plane(core_row)).wait_recv()
-
-    def core_send(i, q):
-        piece = xc.at[q, pl.ds(core * 8 + 1, 8)]
-        send(piece, piece, cc_s.at[i], cc_r.at[i], plane(core_row))
-
-    q_x, q_up, q_down = x_row // 2, yup_row // 2, ydown_row // 2
-    q_xup, q_xdown = ((x_row + 4) % 16) // 2, ((x_row + 12) % 16) // 2
-    q_opp, q_xopp = ((row + 8) % 16) // 2, ((x_row + 8) % 16) // 2
-
-    own_quarter = pq.at[line, own]
-    for i, (a, z) in enumerate(mates):
-        send(own_quarter, own_quarter, gr_s.at[i], gr_r.at[i], {"ep": a, "row": row, "col": z})
-    quarter_spread(0)
     for i in range(15):
         quarter_wait(i)
         quarter_spread(i + 1)

time: 75.8 us -> 73.6 us (0.971)
  Pallas kernels: 75.6 us -> 73.5 us
    pallas_call x1, Pallas kernels: 67.8 us -> 65.6 us  [on_device(): pl.pallas_call(gather_kernel, out_shape=(pltpu.VMEM((1024, 1024), BF16),...]
where the time goes in v3:
time: 73.6 us; the launch traced here: 73.5 us
  Pallas kernels  73.5 us (100%)
    pallas_call x1, Pallas kernels, on_device(): pl.pallas_call(gather_kernel, out_shape=(pltpu.VMEM((1024, 1024), BF16),...  65.6 us
    pallas_call x1, Pallas kernels, on_device(): pl.pallas_call(tile_kernel, grid=(1024 // rows_step,), out_shape=jax.Shap...  7.87 us

profile of v3, /device:TPU:1, one launch (start us, length us, event | category | flops | bytes accessed | tf_op | source)
XLA Modules:
  0.0 73.5 jit_solution(1670863536476913337)
XLA Ops:
  0.0 65.6 %gather.1 = (bf16[1024,1024]{1,0:T(8,128)(2,1)S(1)}, bf16[1024,1024]{1,0:T(8,128)(2,1)S(1)}, f32[1024,512]{1,0:T(8,128)S(1)}, f32[512,1024]{1,0:T(8,128)S(1)}, f32[1,1024]{1,0:T(1,128)S(1)}) custom-call(bf16[64,1024]{1,0:T(8,128)(2,1)} %design_in.1, f32[64]{0:T(128)} %taps_in.1, s32[1,64]{1,0:T(1,128)} %bitcast.5, s32[1,1024]{1,0:T(1,128)} %bitcast.4, ...), custom_call_target="tpu_custom_call" | custom-call | tf_op jit(solution)/shard_map/gather/pallas_call | solution.py:505
  65.6 7.9 %tile.1 = f32[1024,1024]{1,0:T(8,128)} custom-call(bf16[1024,1024]{1,0:T(8,128)(2,1)S(1)} %get-tuple-element.10.frt_ref, bf16[1024,1024]{1,0:T(8,128)(2,1)S(1)} %get-tuple-element.11.fc_ref, f32[1024,512]{1,0:T(8,128)S(1)} %get-tuple-element.12.rr_ref, f32[512,1024]{1,0:T(8,128)S(1)} %get-tuple-element.13.rct_ref, f32[1,1024]{1,0:T(1,128)S(1)} %get-tuple-element.14.reg_ref), custom_call_target="tpu_custom_call" | custom-call | tf_op jit(solution)/shard_map/tile/pallas_call | solution.py:549
